TPU v7x, 256 devices: a whole 4x4x8 slice. The times are simulated.
256 devices in a mesh: dp: 32 (over y, x, core), tensor: 8 (over z).
Axes of the slice: x: 4, y: 4, z: 8, core: 2. Of those that a mesh axis runs over, the one named last changes fastest.
Arguments:
- hidden: bfloat16 [32, 1024, 4096], P('dp', None, 'tensor'), as said below
- gain: float32 [4096], replicated, may hold values from 0.5 to 1.5
- head: bfloat16 [4096, 131072], P(None, ('dp', 'tensor'))
- lengths: int32 [32], P('dp'), may hold values from 256 to 1024, as said below
- offsets: int32 [32, 32], P('dp'), may hold values from 0 to 255
- targets: int32 [32, 32], P('dp'), may hold values from 0 to 131071
- mask: int32 [32, 32], P('dp'), may hold values from 0 to 1, as said below
Outputs:
- logprob: float32 [32, 32], P('dp')
- entropy: float32 [32, 32], P('dp')
Inputs may be any that keep to these rules, and one draw needn't show every extreme that they name: `lengths`: each length is at least 256; some sequence has length exactly 1024 in every draw. `mask`: among the 32 slots of the sequences of one index of dp, at most 16 are scored; some index of dp has exactly 16. `hidden`: entries are of order one or a few tens in magnitude.
All inputs are finite; a program needn't handle non-finite values.
Results may differ from a plain program's by a relative error of at most 0.0089.
Values may be sent and summed in bfloat16 or wider, within the bound.
A program may use at most 64 MiB of HBM per device.

v0:
```python
import jax
import jax.numpy as jnp
from jax import lax
from jax.sharding import PartitionSpec as P


def per_device(hidden, gain, head, lengths, offsets, targets, mask):
    seq_count, slot_count = offsets.shape
    local_rows = seq_count * slot_count
    position = lengths[:, None] - 1 - offsets
    picked = jnp.take_along_axis(hidden, position[:, :, None], axis=1)
    picked = picked.reshape(local_rows, hidden.shape[2])
    full_rows = lax.all_gather(picked, "tensor", axis=1, tiled=True)
    values = full_rows.astype(jnp.float32)
    meansq = jnp.mean(values * values, axis=-1, keepdims=True)
    normed = (values * lax.rsqrt(meansq + 1e-06) * gain).astype(jnp.bfloat16)
    flat_target = targets.reshape(local_rows)
    flat_mask = mask.reshape(local_rows)
    block_rows = normed.shape[0]
    vocab_width = head.shape[1]
    vocab_start = (
        lax.axis_index("dp") * lax.axis_size("tensor") + lax.axis_index("tensor")
    ) * vocab_width
    columns = jnp.arange(vocab_width, dtype=jnp.int32)
    rows_piece = lax.all_gather(normed, "dp", axis=0, tiled=True)
    target_piece = lax.all_gather(flat_target, "dp", axis=0, tiled=True)
    logits = jnp.dot(rows_piece, head, preferred_element_type=jnp.float32)
    top = jnp.max(logits, axis=-1)
    expo = jnp.exp(logits - top[:, None])
    total = jnp.sum(expo, axis=-1)
    weighted = jnp.sum(expo * logits, axis=-1)
    hit = columns[None, :] == (target_piece - vocab_start)[:, None]
    chosen = jnp.sum(jnp.where(hit, logits, 0.0), axis=-1)
    fresh = (top, total, weighted, chosen)
    stats = tuple((new for new in fresh))
    top = lax.pmax(stats[0], ("dp", "tensor"))
    factor = jnp.exp(stats[0] - top)
    total, weighted, chosen = lax.psum(
        (stats[1] * factor, stats[2] * factor, stats[3]), ("dp", "tensor")
    )
    lse = top + jnp.log(total)
    score = chosen - lse
    spread = lse - weighted / total
    offset_rows = lax.axis_index("dp") * block_rows
    score = lax.dynamic_slice_in_dim(score, offset_rows, block_rows)
    spread = lax.dynamic_slice_in_dim(spread, offset_rows, block_rows)
    keep = flat_mask.astype(jnp.float32)
    logprob = (keep * score).reshape(seq_count, slot_count)
    entropy = (keep * spread).reshape(seq_count, slot_count)
    return (logprob, entropy)


def solution(mesh):
    return jax.shard_map(
        per_device,
        mesh=mesh,
        in_specs=(
            P("dp", None, "tensor"),
            P(),
            P(None, ("dp", "tensor")),
            P("dp"),
            P("dp", None),
            P("dp", None),
            P("dp", None),
        ),
        out_specs=(P("dp", None), P("dp", None)),
        check_vma=False,
    )
```

profile of v0, /device:TPU:1, one launch (start us, length us, event | category | flops | bytes accessed | tf_op | source)
XLA Modules:
  0.0 265.7 jit_solution(5815184149624589043)
XLA Ops:
  7.2 0.0 copy-start
  7.2 0.0 all-gather.3.cloned.1.call-start
  7.9 0.7 fusion.7
  8.6 0.7 compare_and_fusion
  9.3 0.0 copy-done
  9.3 0.6 gather_fusion
  9.9 0.1 broadcast_select_fusion
  10.0 23.3 %all_gather.10 = bf16[32,4096]{1,0:T(8,128)(2,1)S(1)} all-gather(bf16[32,512]{1,0:T(8,128)(2,1)S(1)} %broadcast_select_fusion), channel_id=1, replica_groups=mesh['dp'=32,'tensor'=8] {'tensor'}, dimensions={1}, use_global_device_ids=true | all-gather | bytes 294912 | tf_op jit(solution)/shard_map/all_gather | solution.py:13
  33.3 0.2 fusion.1
  33.4 1.6 fusion.3
  35.0 0.0 all-gather.3.cloned.1.call-update
  35.0 1.3 dynamic-slice
  37.0 0.8 bitcast_dynamic-update-slice_fusion
  37.7 19.8 %all-reduce = s32[1024]{0:T(1024)S(1)} all-reduce(s32[1024]{0:T(1024)S(1)} %bitcast_dynamic-update-slice_fusion), channel_id=2, replica_groups=mesh['dp'=32,'tensor'=8] {'dp'}, use_global_device_ids=true, to_apply=%add | all-reduce | flops 1024 | bytes 8192
  57.6 41.2 %all-gather.3.cloned.1.call-done = bf16[1024,4096]{1,0:T(8,128)(2,1)} async-done(((bf16[32,4096]{1,0:T(8,128)(2,1)}), bf16[1024,4096]{1,0:T(8,128)(2,1)}) %all-gather.3.cloned.1.call-update) | async-done | bytes 8388624 | tf_op jit(solution)/shard_map/all_gather | solution.py:25
  98.8 8.3 %fusion.10 = (f32[1024]{0:T(1024)S(1)}, f32[1024,512]{0,1:T(8,128)S(1)}) fusion(bf16[1024,4096]{1,0:T(8,128)(2,1)} %all-gather.3.cloned.1.call-done, bf16[4096,512]{1,0:T(8,128)(2,1)} %param.9), kind=kOutput, calls=%fused_computation.30 | convolution fusion | flops 4295490560 | bytes 14684160 | tf_op jit(solution)/shard_map/dot_general | solution.py:27
  107.1 0.0 copy-start.1
  107.1 75.8 %pmax.7 = f32[1024]{0:T(1024)S(1)} all-reduce(f32[1024]{0:T(1024)S(1)} %get-tuple-element.14), channel_id=1, replica_groups=mesh['dp'=32,'tensor'=8] {'dp','tensor'}, use_global_device_ids=true, to_apply=%region_4.5 | all-reduce | flops 1024 | bytes 8192 | tf_op jit(solution)/shard_map/pmax | solution.py:36
  182.9 0.7 multiply_reduce_fusion
  183.6 74.6 %all-reduce.1 = (f32[1024]{0:T(1024)S(1)}, f32[1024]{0:T(1024)S(1)}, f32[1024]{0:T(1024)S(1)}) all-reduce(f32[1024]{0:T(1024)S(1)} %get-tuple-element.4, f32[1024]{0:T(1024)S(1)} %get-tuple-element.11, f32[1024]{0:T(1024)S(1)} %get-tuple-element.10), channel_id=1, replica_groups=mesh['dp'=32,'tensor'=8] {'dp','tensor'}, use_global_device_ids=true, to_apply=%region_2.3 | all-reduce | flops 3072 | bytes 24576 | tf_op jit(solution)/shard_map/psum | solution.py:38
  258.3 0.0 copy-done.1
  258.3 0.6 fusion.9
  (6 shorter events, 0.0 us)
Async XLA Ops:
  7.2 2.1 copy-start
  7.2 91.7 %all-gather.3.cloned.1.call-start = ((), (), s32[]{:S(2)}) async-start(), calls=%async_computation | async-start | bytes 8650752 | tf_op jit(solution)/shard_map/all_gather | solution.py:25
  107.1 151.1 %copy-start.1 = (s32[1,32]{1,0:T(1,128)S(1)}, s32[1,32]{1,0:T(1,128)}, u32[]{:S(2)}) copy-start(s32[1,32]{1,0:T(1,128)} %param.13) | copy-start | bytes 388
Sparse Core Ops, SparseCore 0:
  35.2 63.6 all-gather.2
where the time goes:
time: 266 us
  blocking collectives  194 us (73%)
  waiting for transfers between devices  41.3 us (16%)
  between operations  15.5 us (6%)
  matrix products  8.27 us (3%)
  other arithmetic  4.44 us (2%)
  local copies, waits for them, and re-layouts  2.68 us (1%)
    pmax x1, blocking collectives, per_device(): top = lax.pmax(stats[0], ('dp', 'tensor'))  75.8 us
    psum x1, blocking collectives, per_device(): lax.psum((stats[1] * factor, stats[2] * factor, stats[3]), ('dp', 'tensor'))  74.6 us
    all_gather x1, waiting for transfers between devices, per_device(): rows_piece = lax.all_gather(normed, 'dp', axis=0, tiled=True)  41.2 us
    all_gather x1, blocking collectives, per_device(): full_rows = lax.all_gather(picked, 'tensor', axis=1, tiled=True)  23.3 us
    unnamed x1, blocking collectives  19.8 us
    dot_general x1, matrix products, per_device(): logits = jnp.dot(rows_piece, head, preferred_element_type=jnp.float32)  8.27 us
  transfers between devices with their start and end apart: 1, of which 1 were waited for; matrix products, arithmetic and copies ran while one was open for 1% of the time, Pallas kernels for 0%

commit v1 on v0

--- a/solution.py
+++ b/solution.py
@@ -22,7 +22,12 @@
         lax.axis_index("dp") * lax.axis_size("tensor") + lax.axis_index("tensor")
     ) * vocab_width
     columns = jnp.arange(vocab_width, dtype=jnp.int32)
-    rows_piece = lax.all_gather(normed, "dp", axis=0, tiled=True)
+    bank = []
+    for _ in range(lax.psum(1, "dp")):
+        bank.append(normed)
+    rows_piece = jnp.concatenate(
+        lax.all_to_all(jnp.stack(bank, 0), axis_name="dp", split_axis=0, concat_axis=0), 0
+    )
     target_piece = lax.all_gather(flat_target, "dp", axis=0, tiled=True)
     logits = jnp.dot(rows_piece, head, preferred_element_type=jnp.float32)
     top = jnp.max(logits, axis=-1)

time: 266 us -> 315 us (1.18)
  blocking collectives: 194 us -> 281 us
  waiting for transfers between devices: 41.3 us -> 0.01 us
  starting transfers between devices: 0.04 us -> 14.1 us
  between operations: 15.5 us -> 2.11 us
    unnamed x1, blocking collectives: 19.8 us -> 108 us
    all_gather x1 -> x0, waiting for transfers between devices: 41.2 us -> none  [per_device(): rows_piece = lax.all_gather(normed, 'dp', axis=0, tiled=True)]
    all_to_all x0 -> x1, starting transfers between devices: none -> 14.1 us  [per_device(): lax.all_to_all(jnp.stack(bank, 0), axis_name='dp', split_axis=0, concat_a...]
    another operation x0 -> x1, local copies, waits for them, and re-layouts: none -> 4.26 us  [per_device(): jnp.stack(bank, 0)]
  transfers between devices with their start and end apart: 1 -> 1, of which waited for: 1 -> 0; matrix products, arithmetic and copies ran while one was open for 1% -> 0% of each run, Pallas kernels for 0% -> 0%
where the time goes in v1:
time: 315 us
  blocking collectives  281 us (89%)
  starting transfers between devices  14.1 us (4%)
  matrix products  8.28 us (3%)
  local copies, waits for them, and re-layouts  5.61 us (2%)
  other arithmetic  3.73 us (1%)
    unnamed x1, blocking collectives  108 us
    pmax x1, blocking collectives, per_device(): top = lax.pmax(stats[0], ('dp', 'tensor'))  77.1 us
    psum x1, blocking collectives, per_device(): lax.psum((stats[1] * factor, stats[2] * factor, stats[3]), ('dp', 'tensor'))  72.7 us
    all_gather x1, blocking collectives, per_device(): full_rows = lax.all_gather(picked, 'tensor', axis=1, tiled=True)  23.3 us
    all_to_all x1, starting transfers between devices, per_device(): lax.all_to_all(jnp.stack(bank, 0), axis_name='dp', split_axis=0, concat_a...  14.1 us
    dot_general x1, matrix products, per_device(): logits = jnp.dot(rows_piece, head, preferred_element_type=jnp.float32)  8.28 us
  transfers between devices with their start and end apart: 1, of which 0 were waited for; matrix products, arithmetic and copies ran while one was open for 0% of the time, Pallas kernels for 0%

profile of v1, /device:TPU:1, one launch (start us, length us, event | category | flops | bytes accessed | tf_op | source)
XLA Modules:
  0.0 314.5 jit_solution(6621209808135955841)
XLA Ops:
  0.6 0.0 copy-start
  1.4 0.7 fusion.7
  2.0 0.7 compare_and_fusion
  2.7 0.0 copy-done
  2.7 0.6 gather_fusion
  3.4 0.1 broadcast_select_fusion
  3.4 23.3 %all_gather.7 = bf16[32,4096]{1,0:T(8,128)(2,1)S(1)} all-gather(bf16[32,512]{1,0:T(8,128)(2,1)S(1)} %broadcast_select_fusion), channel_id=1, replica_groups=mesh['dp'=32,'tensor'=8] {'tensor'}, dimensions={1}, use_global_device_ids=true | all-gather | bytes 294912 | tf_op jit(solution)/shard_map/all_gather | solution.py:13
  26.7 0.2 fusion.1
  26.9 0.9 fusion.3
  27.7 4.3 %stack.2 = bf16[32,32,4096]{2,1,0:T(8,128)(2,1)} broadcast(bf16[32,4096]{1,0:T(8,128)(2,1)S(1)} %fusion.3), dimensions={1,2} | broadcast | bytes 8650752 | tf_op jit(solution)/shard_map/stack | solution.py:29
  32.0 0.0 copy-start.3
  32.0 0.0 copy-start.2
  32.0 14.1 %all-to-all-start = ((bf16[32,32,4096]{2,1,0:T(8,128)(2,1)}), bf16[32,32,4096]{2,1,0:T(8,128)(2,1)}, u32[]{:S(2)}, u32[]{:S(2)}) async-start(bf16[32,32,4096]{2,1,0:T(8,128)(2,1)} %stack.2), calls=%async_computation | async-start | bytes 16777216 | tf_op jit(solution)/shard_map/all_to_all | solution.py:29
  46.1 0.0 copy-done.3
  46.1 0.6 dynamic-slice
  47.3 0.0 copy-done.2
  47.3 0.1 bitcast_dynamic-update-slice_fusion
  47.5 107.7 %all-reduce = s32[1024]{0:T(1024)S(1)} all-reduce(s32[1024]{0:T(1024)S(1)} %bitcast_dynamic-update-slice_fusion), channel_id=2, replica_groups=mesh['dp'=32,'tensor'=8] {'dp'}, use_global_device_ids=true, to_apply=%add | all-reduce | flops 1024 | bytes 8192
  155.1 0.0 all-to-all-done
  155.1 8.3 %fusion.10 = (f32[1024]{0:T(1024)S(1)}, f32[1024,512]{0,1:T(8,128)S(1)}) fusion(bf16[1024,4096]{1,0:T(8,128)(2,1)} %bitcast.8, bf16[4096,512]{1,0:T(8,128)(2,1)} %param.9), kind=kOutput, calls=%fused_computation.30 | convolution fusion | flops 4295490560 | bytes 14684160 | tf_op jit(solution)/shard_map/dot_general | solution.py:32
  163.4 0.0 copy-start.1
  163.4 77.1 %pmax.7 = f32[1024]{0:T(1024)S(1)} all-reduce(f32[1024]{0:T(1024)S(1)} %get-tuple-element.14), channel_id=1, replica_groups=mesh['dp'=32,'tensor'=8] {'dp','tensor'}, use_global_device_ids=true, to_apply=%region_4.5 | all-reduce | flops 1024 | bytes 8192 | tf_op jit(solution)/shard_map/pmax | solution.py:41
  240.5 0.7 multiply_reduce_fusion
  241.2 72.7 %all-reduce.1 = (f32[1024]{0:T(1024)S(1)}, f32[1024]{0:T(1024)S(1)}, f32[1024]{0:T(1024)S(1)}) all-reduce(f32[1024]{0:T(1024)S(1)} %get-tuple-element.4, f32[1024]{0:T(1024)S(1)} %get-tuple-element.11, f32[1024]{0:T(1024)S(1)} %get-tuple-element.10), channel_id=1, replica_groups=mesh['dp'=32,'tensor'=8] {'dp','tensor'}, use_global_device_ids=true, to_apply=%region_2.3 | all-reduce | flops 3072 | bytes 24576 | tf_op jit(solution)/shard_map/psum | solution.py:43
  313.9 0.0 copy-done.1
  313.9 0.6 fusion.9
  (6 shorter events, 0.0 us)
Async XLA Ops:
  0.6 2.1 copy-start
  32.0 14.1 %copy-start.3 = (u32[256]{0:T(256)S(1)}, u32[256]{0:T(256)}, u32[]{:S(2)}) copy-start(u32[256]{0:T(256)} %constant.53) | copy-start | bytes 3076
  32.0 15.3 %copy-start.2 = (s32[1,32]{1,0:T(1,128)S(1)}, s32[1,32]{1,0:T(1,128)}, u32[]{:S(2)}) copy-start(s32[1,32]{1,0:T(1,128)} %param.12) | copy-start | bytes 388
  32.0 123.1 %all-to-all-start = ((bf16[32,32,4096]{2,1,0:T(8,128)(2,1)}), bf16[32,32,4096]{2,1,0:T(8,128)(2,1)}, u32[]{:S(2)}, u32[]{:S(2)}) async-start(bf16[32,32,4096]{2,1,0:T(8,128)(2,1)} %stack.2), calls=%async_computation | async-start | bytes 16777216 | tf_op jit(solution)/shard_map/all_to_all | solution.py:29
  163.4 150.5 %copy-start.1 = (s32[1,32]{1,0:T(1,128)S(1)}, s32[1,32]{1,0:T(1,128)}, u32[]{:S(2)}) copy-start(s32[1,32]{1,0:T(1,128)} %param.13) | copy-start | bytes 388
